TPU v7x, 32 devices: a whole 2x2x4 slice. The times are simulated.
32 devices in a mesh: dom: 8 (over y, x, core), rep: 4 (over z).
Axes of the slice: x: 2, y: 2, z: 4, core: 2. Of those that a mesh axis runs over, the one named last changes fastest.
Arguments:
- hop_feats: bfloat16 [3, 65536, 128], P(None, ('dom', 'rep')), may hold values from -6 to 6
- adj_local: bfloat16 [512, 12, 128, 128], P(('dom', 'rep')), may hold values from -0.125 to 0.125
- local_cols: int32 [512, 12], P(('dom', 'rep')), may hold values from 0 to 15
- adj_halo: bfloat16 [512, 4, 128, 128], P(('dom', 'rep')), may hold values from -0.125 to 0.125
- halo_cols: int32 [512, 4], P(('dom', 'rep')), may hold values from 0 to 3
- boundary_rows: int32 [32, 512], P(('dom', 'rep')), may hold values from 0 to 2047
- train_ids: int32 [32, 2048], P(('dom', 'rep')), may hold values from 0 to 2047, as said below
- shuffle: int32 [32, 2048], P(('dom', 'rep')), may hold values from 0 to 2047, as said below
- labels: int32 [65536], P(('dom', 'rep')), may hold values from 0 to 171
- labelled: int32 [65536], P(('dom', 'rep')), may hold values from 0 to 1
- w_first: bfloat16 [512, 1024], P(None, 'rep'), may hold values from -1 to 1
- w_second: bfloat16 [1024, 172], P('rep'), may hold values from -2 to 2
Outputs:
- next_hop: bfloat16 [65536, 128], P(('dom', 'rep'))
- batch_loss: float32 [32, 32], P(('dom', 'rep'))
- grad_first: float32 [512, 1024], P('dom', 'rep')
- grad_second: float32 [1024, 172], P('rep')
Inputs may be any that keep to these rules, and one draw needn't show every extreme that they name: `local_cols`: local tile indices of the partition's own row tiles. `halo_cols`: indices of received boundary tiles. `boundary_rows`: rows of the sending partition itself. `train_ids`: rows of the partition itself. `shuffle`: each row is a permutation of 0 .. 2047.
All inputs are finite; a program needn't handle non-finite values.
Results may differ from a plain program's by a relative error of at most 0.005.
The roundings to bfloat16 on the way count: a program that leaves them out, or rounds other values in their place, can miss the bound.
Values may be sent and summed in bfloat16 or wider, within the bound.
No kernel may reach another device: no remote copies, remote signals or barrier semaphores. Data moves between devices by JAX's collectives and lax.ppermute only.
A program may use at most 128 MiB of HBM per device.

v0:
```python
import jax
import jax.numpy as jnp
from jax import lax
from jax.sharding import PartitionSpec as P


def loss_head(logits, targets, weights_row):
    row_max = jnp.max(logits, axis=1, keepdims=True)
    expos = jnp.exp(logits - row_max)
    totals = jnp.sum(expos, axis=1, keepdims=True)
    classes = lax.broadcasted_iota(jnp.int32, logits.shape, 1)
    onehot = (classes == targets[:, None]).astype(jnp.float32)
    cross = jnp.log(totals[:, 0]) + row_max[:, 0] - jnp.sum(onehot * logits, axis=1)
    count = jnp.maximum(jnp.sum(weights_row), 1.0)
    dlogits = ((expos / totals - onehot) * (weights_row / count)[:, None]).astype(jnp.bfloat16)
    return (cross, dlogits)


def source_losses(cross, weights_row, groups):
    masks = weights_row.reshape(groups, -1)
    sums = jnp.sum(masks * cross.reshape(groups, -1), axis=1)
    return sums / jnp.maximum(jnp.sum(masks, axis=1), 1.0)


def batch_norm(pre):
    center = pre - jnp.mean(pre, axis=-2, keepdims=True)
    rstd = lax.rsqrt(jnp.mean(center * center, axis=-2, keepdims=True) + 1e-05)
    return (center * rstd, rstd)


def norm_back(grad, normed, rstd):
    mean_grad = jnp.mean(grad, axis=-2, keepdims=True)
    mean_proj = jnp.mean(grad * normed, axis=-2, keepdims=True)
    return (grad - mean_grad - normed * mean_proj) * rstd


def contract_rows(left, right):
    return lax.dot_general(
        left, right, (((0,), (0,)), ((), ())), preferred_element_type=jnp.float32
    )


def shards(
    hop_feats,
    adj_local,
    local_cols,
    adj_halo,
    halo_cols,
    boundary_rows,
    train_ids,
    shuffle,
    labels,
    labelled,
    w_first,
    w_second,
):
    num_dom = lax.axis_size("dom")
    num_rep = lax.axis_size("rep")
    devices = num_dom * num_rep
    tile = adj_local.shape[-1]
    row_tiles = adj_local.shape[0]
    rows = row_tiles * tile
    width = hop_feats.shape[2]
    hop_two = hop_feats[2]
    sent = jnp.take(hop_two, boundary_rows[0], axis=0)
    halo = lax.all_to_all(sent, ("dom", "rep"), split_axis=0, concat_axis=0, tiled=True)
    halo_count = halo.shape[0] // tile
    own_tiles = hop_two.reshape(row_tiles, tile, width)
    near = jnp.take(own_tiles, local_cols, axis=0)
    summed = jnp.einsum("ikab,ikbc->iac", adj_local, near, preferred_element_type=jnp.float32)
    far = jnp.take(halo.reshape(halo_count, tile, width), halo_cols, axis=0)
    summed = summed + jnp.einsum(
        "ikab,ikbc->iac", adj_halo, far, preferred_element_type=jnp.float32
    )
    next_hop = summed.reshape(rows, width).astype(jnp.bfloat16)
    order = jnp.take(train_ids[0], shuffle[0], axis=0)
    allfeat = jnp.concatenate([hop_feats[0], hop_feats[1], hop_two, next_hop], axis=1)
    feats = jnp.take(allfeat, order, axis=0)
    own_labels = jnp.take(labels, order, axis=0)
    own_marks = jnp.take(labelled, order, axis=0)
    target_pair = jnp.stack([own_labels, own_marks], axis=0)
    batch = lax.all_to_all(feats, ("dom", "rep"), split_axis=0, concat_axis=0, tiled=True)
    got_pair = lax.all_to_all(target_pair, ("dom", "rep"), split_axis=1, concat_axis=1, tiled=True)
    targets = got_pair[0]
    weights_row = got_pair[1].astype(jnp.float32)
    first_whole, second_whole = (
        lax.all_gather(w_first, "rep", axis=1, tiled=True),
        lax.all_gather(w_second, "rep", axis=0, tiled=True),
    )
    hidden_pre = jnp.dot(batch, first_whole, preferred_element_type=jnp.float32)
    normed, rstd = batch_norm(hidden_pre)
    hidden = jnp.maximum(normed, 0.0).astype(jnp.bfloat16)
    logits = jnp.dot(hidden, second_whole, preferred_element_type=jnp.float32)
    cross, dlogits = loss_head(logits, targets, weights_row)
    grad_two_full = contract_rows(hidden, dlogits)
    dhidden = lax.dot_general(
        dlogits, second_whole, (((1,), (1,)), ((), ())), preferred_element_type=jnp.float32
    )
    masked = jnp.where(normed > 0, dhidden, 0.0)
    dpre = norm_back(masked, normed, rstd).astype(jnp.bfloat16)
    grad_one_full = contract_rows(batch, dpre)
    grad_one_rep, grad_two_rep = (
        lax.psum_scatter(grad_one_full, "rep", scatter_dimension=1, tiled=True),
        lax.psum_scatter(grad_two_full, "rep", scatter_dimension=0, tiled=True),
    )
    grad_one = lax.psum_scatter(grad_one_rep, "dom", scatter_dimension=0, tiled=True)
    grad_two = lax.psum(grad_two_rep, "dom")
    loss = source_losses(cross, weights_row, devices)
    return (next_hop, loss.reshape(1, devices), grad_one, grad_two)


def solution(mesh):
    placed = (
        P(None, ("dom", "rep"), None),
        P(("dom", "rep"), None, None, None),
        P(("dom", "rep"), None),
        P(("dom", "rep"), None, None, None),
        P(("dom", "rep"), None),
        P(("dom", "rep"), None),
        P(("dom", "rep"), None),
        P(("dom", "rep"), None),
        P(("dom", "rep")),
        P(("dom", "rep")),
        P(None, "rep"),
        P("rep", None),
    )
    return jax.shard_map(
        shards,
        mesh=mesh,
        in_specs=placed,
        out_specs=(
            P(("dom", "rep"), None),
            P(("dom", "rep"), None),
            P("dom", "rep"),
            P("rep", None),
        ),
        check_vma=False,
    )
```

profile of v0, /device:TPU:0, one launch (start us, length us, event | category | flops | bytes accessed | tf_op | source)
XLA Modules:
  0.0 375.0 jit_solution(16362593156664925678)
XLA Ops:
  7.2 0.8 compare_select_fusion.5
  8.5 1.3 reduce.13
  10.0 2.6 slice_bitcast_fusion.1
  12.7 1.3 gather_fusion.1
  14.0 0.8 broadcast_select_fusion.1
  14.8 7.3 %all-to-all-start = ((bf16[32,16,128]{2,1,0:T(8,128)(2,1)}), bf16[32,16,128]{2,1,0:T(8,128)(2,1)S(1)}, u32[]{:S(2)}, u32[]{:S(2)}) async-start(bf16[32,16,128]{2,1,0:T(8,128)(2,1)} %broadcast_select_fusion.1), calls=%async_computation | async-start | bytes 262144 | tf_op jit(solution)/shard_map/all_to_all | solution.py:66
  22.4 11.8 %gather_fusion.4 = s32[2048]{0:T(1024)S(1)} fusion(s32[2048]{0:T(1024)S(1)} %bitcast.44, s32[2048]{0:T(1024)S(1)} %fusion.25), kind=kCustom, calls=%fused_computation.clone | custom fusion | bytes 24576 | tf_op jit(solution)/shard_map/jit(_take)/gather | solution.py:76
  34.9 11.8 %gather_fusion.6 = s32[2048]{0:T(1024)S(1)} fusion(s32[2048]{0:T(1024)S(1)} %copy-done.2, s32[2048]{0:T(1024)S(1)} %broadcast_clamp_fusion), kind=kCustom, calls=%fused_computation.2.clone | custom fusion | bytes 24576 | tf_op jit(solution)/shard_map/jit(_take)/gather | solution.py:80
  46.7 11.8 %gather_fusion.5 = s32[2048]{0:T(1024)S(1)} fusion(s32[2048]{0:T(1024)S(1)} %copy-done.3, s32[2048]{0:T(1024)S(1)} %broadcast_clamp_fusion), kind=kCustom, calls=%fused_computation.1.clone | custom fusion | bytes 24576 | tf_op jit(solution)/shard_map/jit(_take)/gather | solution.py:79
  59.7 8.0 %gather_fusion = bf16[192,128,128]{2,1,0:T(8,128)(2,1)} fusion(bf16[16,128,128]{2,1,0:T(8,128)(2,1)S(1)} %bitcast.45, s32[1024]{0:T(1024)S(1)} %pad_clamp_fusion.2), kind=kCustom, calls=%fused_computation.3 | custom fusion | bytes 12583680 | tf_op jit(solution)/shard_map/jit(_take)/gather | solution.py:69
  67.7 5.8 %all-to-all-start.1 = ((s32[32,1,128]{2,1,0:T(1,128)}), s32[32,1,128]{2,1,0:T(1,128)S(1)}, u32[]{:S(2)}, u32[]{:S(2)}) async-start(s32[32,1,128]{2,1,0:T(1,128)} %reshape.253), calls=%async_computation.1 | async-start | bytes 32768 | tf_op jit(solution)/shard_map/all_to_all | solution.py:83
  73.6 2.2 gather_fusion.2
  75.8 2.4 fusion.9
  78.2 6.6 %fusion.18 = bf16[16,128,128]{1,2,0:T(8,128)(2,1)S(1)} fusion(f32[16,128,128]{1,2,0:T(8,128)S(1)} %fusion.9, bf16[16,12,128,128]{3,2,1,0:T(8,128)(2,1)} %param.15, bf16[16,12,128,128]{3,2,1,0:T(8,128)(2,1)} %bitcast.48, pred[16,12]{1,0:T(8,128)(4,1)S(1)} %compare_and_fusion.2), kind=kOutput, calls=%fused_computation.31 | convolution fusion | flops 808976384 | bytes 14155968 | tf_op jit(solution)/shard_map/ikab,ikbc->iac/dot_general | solution.py:70
  85.5 1.6 pad_maximum_fusion
  87.1 11.1 %gather_fusion.3 = bf16[2048,512]{1,0:T(8,128)(2,1)} fusion(bf16[2048,512]{1,0:T(8,128)(2,1)} %pad_maximum_fusion, s32[2048]{0:T(1024)S(1)} %broadcast_clamp_fusion), kind=kCustom, calls=%fused_computation.6 | custom fusion | bytes 4202496 | tf_op jit(solution)/shard_map/jit(_take)/gather | solution.py:78
  98.2 2.8 broadcast_select_fusion
  101.0 6.0 %all-to-all-start.2 = ((bf16[32,64,512]{2,1,0:T(8,128)(2,1)}), bf16[32,64,512]{2,1,0:T(8,128)(2,1)}, u32[]{:S(2)}, u32[]{:S(2)}) async-start(bf16[32,64,512]{2,1,0:T(8,128)(2,1)} %broadcast_select_fusion), calls=%async_computation.2 | async-start | bytes 4194304 | tf_op jit(solution)/shard_map/all_to_all | solution.py:82
  107.7 73.9 %all_gather.7 = bf16[1024,172]{0,1:T(8,128)(2,1)} all-gather(bf16[256,172]{0,1:T(8,128)(2,1)S(1)} %copy-done.9), channel_id=1, replica_groups=mesh['dom'=8,'rep'=4] {'rep'}, dimensions={0}, use_global_device_ids=true | all-gather | bytes 440320 | tf_op jit(solution)/shard_map/all_gather | solution.py:88
  184.3 0.8 divide_reduce_fusion
  187.1 4.2 %fusion.35 = (f32[1024]{0:T(1024)S(1)}, f32[2048,1024]{1,0:T(8,128)S(1)}) fusion(bf16[2048,512]{1,0:T(8,128)(2,1)} %bitcast.21, bf16[512,1024]{1,0:T(8,128)(2,1)} %all-gather.2.cloned.1.call-done), kind=kOutput, calls=%fused_computation.77 | convolution fusion | flops 2149579776 | bytes 11538432 | tf_op jit(solution)/shard_map/dot_general | solution.py:90
  191.3 0.9 multiply_reduce_fusion.1
  192.6 1.6 fusion.36
  194.2 1.0 fusion.21
  195.8 2.5 fusion.23
  198.3 7.4 %fusion = (f32[1024]{0:T(1024)}, f32[1024]{0:T(1024)}, f32[2048,1024]{1,0:T(8,128)}) fusion(f32[2048,1024]{1,0:T(8,128)} %copy-done.4, f32[1024]{0:T(1024)S(1)} %add_rsqrt_fusion, f32[1024]{0:T(1024)S(1)} %broadcast_multiply_fusion.2, bf16[1024,172]{0,1:T(8,128)(2,1)} %all_gather.7, f32[2048,172]{0,1:T(8,128)S(1)} %get-tuple-element.22, f32[2048]{0:T(1024)} %div.54, ...), kind=kOutput, calls=%fused_computation.13 | convolution fusion | flops 738564096 | bytes 18587648 | tf_op jit(solution)/shard_map/dot_general | solution.py:96
  206.5 10.6 %fusion.4 = f32[512,1024]{1,0:T(8,128)} fusion(bf16[2048,512]{1,0:T(8,128)(2,1)} %bitcast.21, f32[2048,1024]{1,0:T(8,128)} %get-tuple-element.23, f32[2048,1024]{1,0:T(8,128)} %copy-done.4, f32[1024]{0:T(1024)S(1)} %get-tuple-element.24, f32[1024]{0:T(1024)S(1)} %get-tuple-element.25, f32[1024]{0:T(1024)S(1)} %add_rsqrt_fusion, ...), kind=kOutput, calls=%fused_computation.17 | convolution fusion | flops 2166358016 | bytes 20987904 | tf_op jit(solution)/shard_map/dot_general | solution.py:38
  217.2 11.8 %reduce-scatter.8.cloned.1.call-done = f32[256,172]{0,1:T(8,128)} async-done(((f32[1024,172]{0,1:T(8,128)}), f32[256,172]{0,1:T(8,128)}) %reduce-scatter.8.cloned.1.call-update) | async-done | bytes 176144 | tf_op jit(solution)/shard_map/reduce_scatter | solution.py:104
  229.0 44.9 %reduce-scatter.4.cloned.1.call-done = f32[512,256]{1,0:T(8,128)} async-done(((f32[512,1024]{1,0:T(8,128)}), f32[512,256]{1,0:T(8,128)}) %reduce-scatter.4.cloned.1.call-update) | async-done | bytes 524304 | tf_op jit(solution)/shard_map/reduce_scatter | solution.py:103
  274.7 54.4 %all-reduce.2.cloned.1.call-done = f32[256,172]{0,1:T(8,128)} async-done(((f32[256,172]{0,1:T(8,128)}), f32[256,172]{0,1:T(8,128)}) %all-reduce.2.cloned.1.call-update) | async-done | bytes 176144 | tf_op jit(solution)/shard_map/psum | solution.py:107
  329.2 37.7 %reduce-scatter.6.cloned.1.call-done = f32[64,256]{1,0:T(8,128)} async-done(((f32[512,256]{1,0:T(8,128)}), f32[64,256]{1,0:T(8,128)}) %reduce-scatter.6.cloned.1.call-update) | async-done | bytes 65552 | tf_op jit(solution)/shard_map/reduce_scatter | solution.py:106
  366.9 1.6 copy.25
  (91 shorter events, 10.7 us)
Async XLA Ops:
  7.2 68.6 %copy-start = (bf16[16,4,128,128]{3,2,1,0:T(8,128)(2,1)S(1)}, bf16[16,4,128,128]{3,2,1,0:T(8,128)(2,1)}, u32[]{:S(2)}) copy-start(bf16[16,4,128,128]{3,2,1,0:T(8,128)(2,1)} %param.17) | copy-start | bytes 6291460
  10.0 12.1 %copy-start.18 = (s32[16,4]{0,1:T(4,128)S(1)}, s32[16,4]{0,1:T(4,128)}, u32[]{:S(2)}) copy-start(s32[16,4]{0,1:T(4,128)} %param.18) | copy-start | bytes 772
  10.0 12.4 %copy-start.10 = (s32[1,2048]{1,0:T(1,128)S(1)}, s32[1,2048]{1,0:T(1,128)}, u32[]{:S(2)}) copy-start(s32[1,2048]{1,0:T(1,128)} %param.21) | copy-start | bytes 24580
  10.0 12.4 %copy-start.1 = (s32[1,2048]{1,0:T(1,128)S(1)}, s32[1,2048]{1,0:T(1,128)}, u32[]{:S(2)}) copy-start(s32[1,2048]{1,0:T(1,128)} %param.20) | copy-start | bytes 24580
  14.8 53.0 %all-to-all-start = ((bf16[32,16,128]{2,1,0:T(8,128)(2,1)}), bf16[32,16,128]{2,1,0:T(8,128)(2,1)S(1)}, u32[]{:S(2)}, u32[]{:S(2)}) async-start(bf16[32,16,128]{2,1,0:T(8,128)(2,1)} %broadcast_select_fusion.1), calls=%async_computation | async-start | bytes 262144 | tf_op jit(solution)/shard_map/all_to_all | solution.py:66
  34.2 0.7 copy-start.2
  34.9 11.8 %copy-start.3 = (s32[2048]{0:T(1024)S(1)}, s32[2048]{0:T(1024)}, u32[]{:S(2)}) copy-start(s32[2048]{0:T(1024)} %param.22) | copy-start | bytes 24580
  46.7 12.0 %copy-start.16 = (s32[16,12]{1,0:T(8,128)S(1)}, s32[16,12]{1,0:T(8,128)}, u32[]{:S(2)}) copy-start(s32[16,12]{1,0:T(8,128)} %param.16) | copy-start | bytes 2308
  67.7 33.2 %all-to-all-start.1 = ((s32[32,1,128]{2,1,0:T(1,128)}), s32[32,1,128]{2,1,0:T(1,128)S(1)}, u32[]{:S(2)}, u32[]{:S(2)}) async-start(s32[32,1,128]{2,1,0:T(1,128)} %reshape.253), calls=%async_computation.1 | async-start | bytes 32768 | tf_op jit(solution)/shard_map/all_to_all | solution.py:83
  78.1 7.4 %copy-start.5 = (bf16[2048,128]{1,0:T(8,128)(2,1)S(1)}, bf16[2048,128]{1,0:T(8,128)(2,1)}, u32[]{:S(2)}) copy-start(bf16[2048,128]{1,0:T(8,128)(2,1)} %get-tuple-element.13) | copy-start | bytes 1572868
  78.1 7.4 %copy-start.6 = (bf16[2048,128]{1,0:T(8,128)(2,1)S(1)}, bf16[2048,128]{1,0:T(8,128)(2,1)}, u32[]{:S(2)}) copy-start(bf16[2048,128]{1,0:T(8,128)(2,1)} %get-tuple-element.16) | copy-start | bytes 1572868
  84.7 0.8 copy-start.8
  101.0 6.8 %copy-start.9 = (bf16[256,172]{0,1:T(8,128)(2,1)S(1)}, bf16[256,172]{0,1:T(8,128)(2,1)}, u32[]{:S(2)}) copy-start(bf16[256,172]{0,1:T(8,128)(2,1)} %param.25) | copy-start | bytes 264196
  101.0 86.1 %all-to-all-start.2 = ((bf16[32,64,512]{2,1,0:T(8,128)(2,1)}), bf16[32,64,512]{2,1,0:T(8,128)(2,1)}, u32[]{:S(2)}, u32[]{:S(2)}) async-start(bf16[32,64,512]{2,1,0:T(8,128)(2,1)} %broadcast_select_fusion), calls=%async_computation.2 | async-start | bytes 4194304 | tf_op jit(solution)/shard_map/all_to_all | solution.py:82
  107.0 80.1 %all-gather.2.cloned.1.call-start = ((), (), s32[]{:S(2)}) async-start(), calls=%async_computation.6 | async-start | bytes 1310720 | tf_op jit(solution)/shard_map/all_gather | solution.py:87
  107.7 121.3 %reduce-scatter.8.cloned.1.call-start = ((), (), s32[]{:S(2)}) async-start(), calls=%async_computation.9 | async-start | bytes 901120 | tf_op jit(solution)/shard_map/reduce_scatter | solution.py:104
  191.3 3.9 %copy-start.4 = (f32[2048,1024]{1,0:T(8,128)}, f32[2048,1024]{1,0:T(8,128)S(1)}, u32[]{:S(2)}) copy-start(f32[2048,1024]{1,0:T(8,128)S(1)} %get-tuple-element.20) | copy-start | bytes 25165828
  191.3 1.3 copy-start.7
  192.6 1.6 copy-start.12
  192.6 3.2 copy-start.17
  195.2 0.6 copy-start.13
  205.7 68.2 %reduce-scatter.4.cloned.1.call-start = ((), (), s32[]{:S(2)}) async-start(), calls=%async_computation.7 | async-start | bytes 2621440 | tf_op jit(solution)/shard_map/reduce_scatter | solution.py:103
  217.1 56.9 %copy-start.14 = (f32[2048]{0:T(1024)S(1)}, f32[2048]{0:T(1024)}, u32[]{:S(2)}) copy-start(f32[2048]{0:T(1024)} %copy-done.13) | copy-start | bytes 24580
  217.1 56.9 %copy-start.15 = (f32[2048]{0:T(1024)S(1)}, f32[2048]{0:T(1024)}, u32[]{:S(2)}) copy-start(f32[2048]{0:T(1024)} %get-tuple-element.8) | copy-start | bytes 24580
  217.1 57.0 %copy-start.11 = (f32[1,32,64]{2,0,1:T(1,128)S(1)}, f32[1,32,64]{2,0,1:T(1,128)}, u32[]{:S(2)}) copy-start(f32[1,32,64]{2,0,1:T(1,128)} %get-tuple-element.18) | copy-start | bytes 24580
  217.1 57.1 %copy-start.19 = (f32[32]{0:T(128)S(1)}, f32[32]{0:T(128)}, u32[]{:S(2)}) copy-start(f32[32]{0:T(128)} %get-tuple-element.10) | copy-start | bytes 388
  217.1 112.0 %all-reduce.2.cloned.1.call-start = ((), (), s32[]{:S(2)}) async-start(), calls=%async_computation.10 | async-start | bytes 360448 | tf_op jit(solution)/shard_map/psum | solution.py:107
  229.0 137.9 %reduce-scatter.6.cloned.1.call-start = ((), (), s32[]{:S(2)}) async-start(), calls=%async_computation.8 | async-start | bytes 589824 | tf_op jit(solution)/shard_map/reduce_scatter | solution.py:106
Sparse Core Ops, SparseCore 0:
  109.3 55.8 all-gather.1
  205.8 23.0 reduce-scatter.7
  231.2 42.6 reduce-scatter.3
  276.9 52.1 all-reduce.1
  332.6 34.2 reduce-scatter.5
where the time goes:
time: 376 us; the launch traced here: 375 us
  waiting for transfers between devices  150 us (40%)
  blocking collectives  73.9 us (20%)
  local copies, waits for them, and re-layouts  68.5 us (18%)
  matrix products  35.3 us (9%)
  starting transfers between devices  19.3 us (5%)
  between operations  14.8 us (4%)
  other arithmetic  13.5 us (4%)
    all_gather x1, blocking collectives, shards(): lax.all_gather(w_second, 'rep', axis=0, tiled=True)  73.9 us
    psum x1, waiting for transfers between devices, shards(): grad_two = lax.psum(grad_two_rep, 'dom')  54.4 us
    reduce_scatter x1, waiting for transfers between devices, shards(): lax.psum_scatter(grad_one_full, 'rep', scatter_dimension=1, tiled=True)  44.9 us
    reduce_scatter x1, waiting for transfers between devices, shards(): lax.psum_scatter(grad_one_rep, 'dom', scatter_dimension=0, tiled=True)  37.7 us
    dot_general x2, matrix products, contract_rows(): lax.dot_general(left, right, (((0,), (0,)), ((), ())), preferred_element_...  13.2 us
    gather x1, local copies, waits for them, and re-layouts, shards(): order = jnp.take(train_ids[0], shuffle[0], axis=0)  11.8 us
    gather x1, local copies, waits for them, and re-layouts, shards(): own_labels = jnp.take(labels, order, axis=0)  11.8 us
    gather x1, local copies, waits for them, and re-layouts, shards(): own_marks = jnp.take(labelled, order, axis=0)  11.8 us
  transfers between devices with their start and end apart: 8, of which 4 were waited for; matrix products, arithmetic and copies ran while one was open for 23% of the time, Pallas kernels for 0%

commit v1 on v0

--- a/solution.py
+++ b/solution.py
@@ -104,7 +104,8 @@
         lax.psum_scatter(grad_two_full, "rep", scatter_dimension=0, tiled=True),
     )
     grad_one = lax.psum_scatter(grad_one_rep, "dom", scatter_dimension=0, tiled=True)
-    grad_two = lax.psum(grad_two_rep, "dom")
+    parts = lax.all_gather(grad_two_rep, "dom", axis=0, tiled=False)
+    grad_two = parts.sum(axis=0)
     loss = source_losses(cross, weights_row, devices)
     return (next_hop, loss.reshape(1, devices), grad_one, grad_two)
 

time: 376 us -> 345 us (0.918)
  waiting for transfers between devices: 150 us -> 118 us
    psum x1 -> x0, waiting for transfers between devices: 54.4 us -> none  [shards(): grad_two = lax.psum(grad_two_rep, 'dom')]
    all_gather x0 -> x1, waiting for transfers between devices: none -> 25.4 us  [shards(): parts = lax.all_gather(grad_two_rep, 'dom', axis=0, tiled=False)]
  transfers between devices with their start and end apart: 8 -> 8, of which waited for: 4 -> 4; matrix products, arithmetic and copies ran while one was open for 23% -> 26% of each run, Pallas kernels for 0% -> 0%
where the time goes in v1:
time: 345 us; the launch traced here: 344 us
  waiting for transfers between devices  118 us (34%)
  blocking collectives  73.9 us (21%)
  local copies, waits for them, and re-layouts  68.8 us (20%)
  matrix products  35.3 us (10%)
  starting transfers between devices  19.3 us (6%)
  between operations  14.8 us (4%)
  other arithmetic  14.5 us (4%)
    all_gather x1, blocking collectives, shards(): lax.all_gather(w_second, 'rep', axis=0, tiled=True)  73.9 us
    reduce_scatter x1, waiting for transfers between devices, shards(): lax.psum_scatter(grad_one_full, 'rep', scatter_dimension=1, tiled=True)  44.9 us
    reduce_scatter x1, waiting for transfers between devices, shards(): lax.psum_scatter(grad_one_rep, 'dom', scatter_dimension=0, tiled=True)  34.7 us
    all_gather x1, waiting for transfers between devices, shards(): parts = lax.all_gather(grad_two_rep, 'dom', axis=0, tiled=False)  25.4 us
    dot_general x2, matrix products, contract_rows(): lax.dot_general(left, right, (((0,), (0,)), ((), ())), preferred_element_...  13.2 us
    gather x1, local copies, waits for them, and re-layouts, shards(): order = jnp.take(train_ids[0], shuffle[0], axis=0)  11.8 us
    gather x1, local copies, waits for them, and re-layouts, shards(): own_labels = jnp.take(labels, order, axis=0)  11.8 us
    gather x1, local copies, waits for them, and re-layouts, shards(): own_marks = jnp.take(labelled, order, axis=0)  11.8 us
  transfers between devices with their start and end apart: 8, of which 4 were waited for; matrix products, arithmetic and copies ran while one was open for 26% of the time, Pallas kernels for 0%

profile of v1, /device:TPU:0, one launch (start us, length us, event | category | flops | bytes accessed | tf_op | source)
XLA Modules:
  0.0 344.3 jit_solution(5102519077817672114)
XLA Ops:
  7.2 0.8 compare_select_fusion.5
  8.5 1.3 reduce.13
  10.0 2.6 slice_bitcast_fusion.1
  12.7 1.3 gather_fusion.1
  14.8 7.3 %all-to-all-start = ((bf16[32,16,128]{2,1,0:T(8,128)(2,1)}), bf16[32,16,128]{2,1,0:T(8,128)(2,1)S(1)}, u32[]{:S(2)}, u32[]{:S(2)}) async-start(bf16[32,16,128]{2,1,0:T(8,128)(2,1)} %broadcast_select_fusion.1), calls=%async_computation | async-start | bytes 262144 | tf_op jit(solution)/shard_map/all_to_all | solution.py:66
  22.4 11.8 %gather_fusion.4 = s32[2048]{0:T(1024)S(1)} fusion(s32[2048]{0:T(1024)S(1)} %bitcast.50, s32[2048]{0:T(1024)S(1)} %fusion.25), kind=kCustom, calls=%fused_computation.clone | custom fusion | bytes 24576 | tf_op jit(solution)/shard_map/jit(_take)/gather | solution.py:76
  34.9 11.8 %gather_fusion.6 = s32[2048]{0:T(1024)S(1)} fusion(s32[2048]{0:T(1024)S(1)} %copy-done.2, s32[2048]{0:T(1024)S(1)} %broadcast_clamp_fusion), kind=kCustom, calls=%fused_computation.2.clone | custom fusion | bytes 24576 | tf_op jit(solution)/shard_map/jit(_take)/gather | solution.py:80
  46.7 11.8 %gather_fusion.5 = s32[2048]{0:T(1024)S(1)} fusion(s32[2048]{0:T(1024)S(1)} %copy-done.3, s32[2048]{0:T(1024)S(1)} %broadcast_clamp_fusion), kind=kCustom, calls=%fused_computation.1.clone | custom fusion | bytes 24576 | tf_op jit(solution)/shard_map/jit(_take)/gather | solution.py:79
  59.7 8.0 %gather_fusion = bf16[192,128,128]{2,1,0:T(8,128)(2,1)} fusion(bf16[16,128,128]{2,1,0:T(8,128)(2,1)S(1)} %bitcast.51, s32[1024]{0:T(1024)S(1)} %pad_clamp_fusion.2), kind=kCustom, calls=%fused_computation.3 | custom fusion | bytes 12583680 | tf_op jit(solution)/shard_map/jit(_take)/gather | solution.py:69
  67.7 5.8 %all-to-all-start.1 = ((s32[32,1,128]{2,1,0:T(1,128)}), s32[32,1,128]{2,1,0:T(1,128)S(1)}, u32[]{:S(2)}, u32[]{:S(2)}) async-start(s32[32,1,128]{2,1,0:T(1,128)} %reshape.254), calls=%async_computation.1 | async-start | bytes 32768 | tf_op jit(solution)/shard_map/all_to_all | solution.py:83
  73.6 2.2 gather_fusion.2
  75.8 2.4 fusion.9
  78.2 6.6 %fusion.18 = bf16[16,128,128]{1,2,0:T(8,128)(2,1)S(1)} fusion(f32[16,128,128]{1,2,0:T(8,128)S(1)} %fusion.9, bf16[16,12,128,128]{3,2,1,0:T(8,128)(2,1)} %param.15, bf16[16,12,128,128]{3,2,1,0:T(8,128)(2,1)} %bitcast.54, pred[16,12]{1,0:T(8,128)(4,1)S(1)} %compare_and_fusion.2), kind=kOutput, calls=%fused_computation.32 | convolution fusion | flops 808976384 | bytes 14155968 | tf_op jit(solution)/shard_map/ikab,ikbc->iac/dot_general | solution.py:70
  85.5 1.6 pad_maximum_fusion
  87.1 11.1 %gather_fusion.3 = bf16[2048,512]{1,0:T(8,128)(2,1)} fusion(bf16[2048,512]{1,0:T(8,128)(2,1)} %pad_maximum_fusion, s32[2048]{0:T(1024)S(1)} %broadcast_clamp_fusion), kind=kCustom, calls=%fused_computation.6 | custom fusion | bytes 4202496 | tf_op jit(solution)/shard_map/jit(_take)/gather | solution.py:78
  98.2 2.8 broadcast_select_fusion
  101.0 6.0 %all-to-all-start.2 = ((bf16[32,64,512]{2,1,0:T(8,128)(2,1)}), bf16[32,64,512]{2,1,0:T(8,128)(2,1)}, u32[]{:S(2)}, u32[]{:S(2)}) async-start(bf16[32,64,512]{2,1,0:T(8,128)(2,1)} %broadcast_select_fusion), calls=%async_computation.2 | async-start | bytes 4194304 | tf_op jit(solution)/shard_map/all_to_all | solution.py:82
  107.7 73.9 %all_gather.13 = bf16[1024,172]{0,1:T(8,128)(2,1)} all-gather(bf16[256,172]{0,1:T(8,128)(2,1)S(1)} %copy-done.9), channel_id=1, replica_groups=mesh['dom'=8,'rep'=4] {'rep'}, dimensions={0}, use_global_device_ids=true | all-gather | bytes 440320 | tf_op jit(solution)/shard_map/all_gather | solution.py:88
  184.3 0.8 divide_reduce_fusion
  187.1 4.2 %fusion.35 = (f32[1024]{0:T(1024)S(1)}, f32[2048,1024]{1,0:T(8,128)S(1)}) fusion(bf16[2048,512]{1,0:T(8,128)(2,1)} %bitcast.21, bf16[512,1024]{1,0:T(8,128)(2,1)} %all-gather.4.cloned.1.call-done), kind=kOutput, calls=%fused_computation.78 | convolution fusion | flops 2149579776 | bytes 11538432 | tf_op jit(solution)/shard_map/dot_general | solution.py:90
  191.3 0.9 multiply_reduce_fusion.1
  192.6 1.6 fusion.36
  194.2 1.0 fusion.21
  195.8 2.5 fusion.23
  198.3 7.4 %fusion = (f32[1024]{0:T(1024)}, f32[1024]{0:T(1024)}, f32[2048,1024]{1,0:T(8,128)}) fusion(f32[2048,1024]{1,0:T(8,128)} %copy-done.4, f32[1024]{0:T(1024)S(1)} %add_rsqrt_fusion, f32[1024]{0:T(1024)S(1)} %broadcast_multiply_fusion.2, bf16[1024,172]{0,1:T(8,128)(2,1)} %all_gather.13, f32[2048,172]{0,1:T(8,128)S(1)} %get-tuple-element.22, f32[2048]{0:T(1024)} %div.54, ...), kind=kOutput, calls=%fused_computation.13 | convolution fusion | flops 738564096 | bytes 18587648 | tf_op jit(solution)/shard_map/dot_general | solution.py:96
  206.5 10.6 %fusion.4 = f32[512,1024]{1,0:T(8,128)} fusion(bf16[2048,512]{1,0:T(8,128)(2,1)} %bitcast.21, f32[2048,1024]{1,0:T(8,128)} %get-tuple-element.23, f32[2048,1024]{1,0:T(8,128)} %copy-done.4, f32[1024]{0:T(1024)S(1)} %get-tuple-element.24, f32[1024]{0:T(1024)S(1)} %get-tuple-element.25, f32[1024]{0:T(1024)S(1)} %add_rsqrt_fusion, ...), kind=kOutput, calls=%fused_computation.17 | convolution fusion | flops 2166358016 | bytes 20987904 | tf_op jit(solution)/shard_map/dot_general | solution.py:38
  217.2 11.8 %reduce-scatter.8.cloned.1.call-done = f32[256,172]{0,1:T(8,128)} async-done(((f32[1024,172]{0,1:T(8,128)}), f32[256,172]{0,1:T(8,128)}) %reduce-scatter.8.cloned.1.call-update) | async-done | bytes 176144 | tf_op jit(solution)/shard_map/reduce_scatter | solution.py:104
  229.0 44.9 %reduce-scatter.4.cloned.1.call-done = f32[512,256]{1,0:T(8,128)} async-done(((f32[512,1024]{1,0:T(8,128)}), f32[512,256]{1,0:T(8,128)}) %reduce-scatter.4.cloned.1.call-update) | async-done | bytes 524304 | tf_op jit(solution)/shard_map/reduce_scatter | solution.py:103
  274.7 25.4 %all-gather.6.cloned.1.call-done = f32[2048,172]{0,1:T(8,128)} async-done(((f32[256,172]{0,1:T(8,128)}), f32[2048,172]{0,1:T(8,128)}) %all-gather.6.cloned.1.call-update) | async-done | bytes 1409040 | tf_op jit(solution)/shard_map/all_gather | solution.py:107
  300.1 1.9 copy.24
  302.0 1.0 bitcast_reduce_fusion
  303.1 34.7 %reduce-scatter.6.cloned.1.call-done = f32[64,256]{1,0:T(8,128)} async-done(((f32[512,256]{1,0:T(8,128)}), f32[64,256]{1,0:T(8,128)}) %reduce-scatter.6.cloned.1.call-update) | async-done | bytes 65552 | tf_op jit(solution)/shard_map/reduce_scatter | solution.py:106
  (92 shorter events, 11.5 us)
Async XLA Ops:
  7.2 68.6 %copy-start = (bf16[16,4,128,128]{3,2,1,0:T(8,128)(2,1)S(1)}, bf16[16,4,128,128]{3,2,1,0:T(8,128)(2,1)}, u32[]{:S(2)}) copy-start(bf16[16,4,128,128]{3,2,1,0:T(8,128)(2,1)} %param.17) | copy-start | bytes 6291460
  10.0 12.1 %copy-start.18 = (s32[16,4]{0,1:T(4,128)S(1)}, s32[16,4]{0,1:T(4,128)}, u32[]{:S(2)}) copy-start(s32[16,4]{0,1:T(4,128)} %param.18) | copy-start | bytes 772
  10.0 12.4 %copy-start.10 = (s32[1,2048]{1,0:T(1,128)S(1)}, s32[1,2048]{1,0:T(1,128)}, u32[]{:S(2)}) copy-start(s32[1,2048]{1,0:T(1,128)} %param.21) | copy-start | bytes 24580
  10.0 12.4 %copy-start.1 = (s32[1,2048]{1,0:T(1,128)S(1)}, s32[1,2048]{1,0:T(1,128)}, u32[]{:S(2)}) copy-start(s32[1,2048]{1,0:T(1,128)} %param.20) | copy-start | bytes 24580
  14.8 53.0 %all-to-all-start = ((bf16[32,16,128]{2,1,0:T(8,128)(2,1)}), bf16[32,16,128]{2,1,0:T(8,128)(2,1)S(1)}, u32[]{:S(2)}, u32[]{:S(2)}) async-start(bf16[32,16,128]{2,1,0:T(8,128)(2,1)} %broadcast_select_fusion.1), calls=%async_computation | async-start | bytes 262144 | tf_op jit(solution)/shard_map/all_to_all | solution.py:66
  34.2 0.7 copy-start.2
  34.9 11.8 %copy-start.3 = (s32[2048]{0:T(1024)S(1)}, s32[2048]{0:T(1024)}, u32[]{:S(2)}) copy-start(s32[2048]{0:T(1024)} %param.22) | copy-start | bytes 24580
  46.7 12.0 %copy-start.16 = (s32[16,12]{1,0:T(8,128)S(1)}, s32[16,12]{1,0:T(8,128)}, u32[]{:S(2)}) copy-start(s32[16,12]{1,0:T(8,128)} %param.16) | copy-start | bytes 2308
  67.7 33.2 %all-to-all-start.1 = ((s32[32,1,128]{2,1,0:T(1,128)}), s32[32,1,128]{2,1,0:T(1,128)S(1)}, u32[]{:S(2)}, u32[]{:S(2)}) async-start(s32[32,1,128]{2,1,0:T(1,128)} %reshape.254), calls=%async_computation.1 | async-start | bytes 32768 | tf_op jit(solution)/shard_map/all_to_all | solution.py:83
  78.1 7.4 %copy-start.5 = (bf16[2048,128]{1,0:T(8,128)(2,1)S(1)}, bf16[2048,128]{1,0:T(8,128)(2,1)}, u32[]{:S(2)}) copy-start(bf16[2048,128]{1,0:T(8,128)(2,1)} %get-tuple-element.13) | copy-start | bytes 1572868
  78.1 7.4 %copy-start.6 = (bf16[2048,128]{1,0:T(8,128)(2,1)S(1)}, bf16[2048,128]{1,0:T(8,128)(2,1)}, u32[]{:S(2)}) copy-start(bf16[2048,128]{1,0:T(8,128)(2,1)} %get-tuple-element.16) | copy-start | bytes 1572868
  84.7 0.8 copy-start.8
  101.0 6.8 %copy-start.9 = (bf16[256,172]{0,1:T(8,128)(2,1)S(1)}, bf16[256,172]{0,1:T(8,128)(2,1)}, u32[]{:S(2)}) copy-start(bf16[256,172]{0,1:T(8,128)(2,1)} %param.25) | copy-start | bytes 264196
  101.0 86.1 %all-to-all-start.2 = ((bf16[32,64,512]{2,1,0:T(8,128)(2,1)}), bf16[32,64,512]{2,1,0:T(8,128)(2,1)}, u32[]{:S(2)}, u32[]{:S(2)}) async-start(bf16[32,64,512]{2,1,0:T(8,128)(2,1)} %broadcast_select_fusion), calls=%async_computation.2 | async-start | bytes 4194304 | tf_op jit(solution)/shard_map/all_to_all | solution.py:82
  107.0 80.1 %all-gather.4.cloned.1.call-start = ((), (), s32[]{:S(2)}) async-start(), calls=%async_computation.6 | async-start | bytes 1310720 | tf_op jit(solution)/shard_map/all_gather | solution.py:87
  107.7 121.3 %reduce-scatter.8.cloned.1.call-start = ((), (), s32[]{:S(2)}) async-start(), calls=%async_computation.9 | async-start | bytes 901120 | tf_op jit(solution)/shard_map/reduce_scatter | solution.py:104
  191.3 3.9 %copy-start.4 = (f32[2048,1024]{1,0:T(8,128)}, f32[2048,1024]{1,0:T(8,128)S(1)}, u32[]{:S(2)}) copy-start(f32[2048,1024]{1,0:T(8,128)S(1)} %get-tuple-element.20) | copy-start | bytes 25165828
  191.3 1.3 copy-start.7
  192.6 1.6 copy-start.12
  192.6 3.2 copy-start.17
  195.2 0.6 copy-start.13
  205.7 68.2 %reduce-scatter.4.cloned.1.call-start = ((), (), s32[]{:S(2)}) async-start(), calls=%async_computation.7 | async-start | bytes 2621440 | tf_op jit(solution)/shard_map/reduce_scatter | solution.py:103
  217.1 56.9 %copy-start.14 = (f32[2048]{0:T(1024)S(1)}, f32[2048]{0:T(1024)}, u32[]{:S(2)}) copy-start(f32[2048]{0:T(1024)} %copy-done.13) | copy-start | bytes 24580
  217.1 56.9 %copy-start.15 = (f32[2048]{0:T(1024)S(1)}, f32[2048]{0:T(1024)}, u32[]{:S(2)}) copy-start(f32[2048]{0:T(1024)} %get-tuple-element.8) | copy-start | bytes 24580
  217.1 57.0 %copy-start.11 = (f32[1,32,64]{2,0,1:T(1,128)S(1)}, f32[1,32,64]{2,0,1:T(1,128)}, u32[]{:S(2)}) copy-start(f32[1,32,64]{2,0,1:T(1,128)} %get-tuple-element.18) | copy-start | bytes 24580
  217.1 57.1 %copy-start.19 = (f32[32]{0:T(128)S(1)}, f32[32]{0:T(128)}, u32[]{:S(2)}) copy-start(f32[32]{0:T(128)} %get-tuple-element.10) | copy-start | bytes 388
  217.1 83.0 %all-gather.6.cloned.1.call-start = ((), (), s32[]{:S(2)}) async-start(), calls=%async_computation.10 | async-start | bytes 1622016 | tf_op jit(solution)/shard_map/all_gather | solution.py:107
  229.0 108.8 %reduce-scatter.6.cloned.1.call-start = ((), (), s32[]{:S(2)}) async-start(), calls=%async_computation.8 | async-start | bytes 589824 | tf_op jit(solution)/shard_map/reduce_scatter | solution.py:106
Sparse Core Ops, SparseCore 0:
  109.3 55.8 all-gather.3
  205.8 23.0 reduce-scatter.7
  231.2 42.6 reduce-scatter.3
  275.7 24.4 all-gather.5
  303.6 34.1 reduce-scatter.5
